TPU v7x, 256 devices: a whole 4x4x8 slice. The times are simulated.
256 devices in a mesh: row: 16 (over z, core), col: 16 (over y, x).
Axes of the slice: x: 4, y: 4, z: 8, core: 2. Of those that a mesh axis runs over, the one named last changes fastest.
Arguments:
- inputs: bfloat16 [2048, 8192], P('col', 'row'), may hold values from -6 to 6
- weight: bfloat16 [8192, 28672], P('row', 'col'), may hold values from -0.09375 to 0.09375
- mask: int32 [64, 224], P('row', 'col'), may hold values 0 or 1
- cotangent: bfloat16 [2048, 28672], P('row', 'col'), may hold values from -6 to 6
Outputs:
- outputs: bfloat16 [2048, 28672], P('row', 'col')
- input_grad: bfloat16 [2048, 8192], P('col', 'row')
- weight_grad: bfloat16 [8192, 28672], P('row', 'col')
Inputs may be any that keep to these rules, and one draw needn't show every extreme that they name: mask holds only zeros and ones.
All inputs are finite; a program needn't handle non-finite values. No bound on the sum of `mask` on one device may be relied on, other than what follows from the above.
Results may differ from a plain program's by a relative error of at most 0.022.
Values may be sent and summed in bfloat16 or wider, within the bound.
A program may use at most 128 MiB of HBM per device.

v0:
```python
import jax
import jax.numpy as jnp
from jax import lax
from jax.sharding import PartitionSpec as P

BLOCK = 128


def expand_mask(mask_tile):
    tile_rows, tile_cols = mask_tile.shape
    mask_bf16 = mask_tile.astype(jnp.bfloat16)
    widened = jnp.broadcast_to(mask_bf16[:, None, :, None], (tile_rows, BLOCK, tile_cols, BLOCK))
    return widened.reshape(tile_rows * BLOCK, tile_cols * BLOCK)


def local(inputs, weight, mask, cotangent):
    keep_mask = expand_mask(mask)
    masked = weight * keep_mask
    whole = lax.all_gather(inputs, "col", axis=0, tiled=True)
    token_total = whole.shape[0]
    chosen = whole
    outputs = lax.psum_scatter(
        jnp.dot(chosen, masked, preferred_element_type=jnp.float32).astype(jnp.bfloat16),
        "row",
        scatter_dimension=0,
        tiled=True,
    )
    shard_rows = lax.all_gather(cotangent, "row", axis=0, tiled=True)
    partial_value = lax.dot_general(
        shard_rows, masked, (((1,), (1,)), ((), ())), preferred_element_type=jnp.float32
    )
    grad_parts = partial_value.astype(jnp.bfloat16)
    chosen = whole
    weight_acc = lax.dot_general(
        chosen, shard_rows, (((0,), (0,)), ((), ())), preferred_element_type=jnp.float32
    )
    grad_parts, weight_acc = (grad_parts, weight_acc)
    summed = lax.psum_scatter(
        grad_parts.astype(jnp.float32).astype(jnp.bfloat16), "col", scatter_dimension=0, tiled=True
    )
    grad_scale = token_total ** (-0.5)
    weight_grad = (weight_acc * keep_mask.astype(jnp.float32) * grad_scale).astype(jnp.bfloat16)
    return (outputs, summed, weight_grad)


def solution(mesh):
    placed = (P("col", "row"), P("row", "col"), P("row", "col"), P("row", "col"))
    return jax.shard_map(
        local,
        mesh=mesh,
        in_specs=placed,
        out_specs=(P("row", "col"), P("col", "row"), P("row", "col")),
        check_vma=False,
    )
```

profile of v0, /device:TPU:10, one launch (start us, length us, event | category | flops | bytes accessed | tf_op | source)
XLA Modules:
  0.0 275.3 jit_solution(2744342380747078628)
XLA Ops:
  7.2 0.0 all-gather.5.cloned.1.call-start
  7.2 0.7 all-gather.5.cloned.1.call-update
  7.9 0.0 all-gather.3.cloned.1.call-start
  7.9 0.7 all-gather.3.cloned.1.call-update
  8.6 0.0 reduce-scatter.9.cloned.1.call-start
  8.7 0.7 convert_element_type.23
  9.4 0.1 copy.14
  9.5 3.8 %copy.15 = bf16[512,1792]{0,1:T(8,128)(2,1)} copy(bf16[512,1792]{1,0:T(8,128)(2,1)} %param.5) | data formatting | bytes 3670016 | tf_op args[1]
  13.3 50.4 %all-gather.5.cloned.1.call-done = bf16[2048,1792]{1,0:T(8,128)(2,1)} async-done(((bf16[128,1792]{1,0:T(8,128)(2,1)}), bf16[2048,1792]{1,0:T(8,128)(2,1)}) %all-gather.5.cloned.1.call-update) | async-done | bytes 7340048 | tf_op jit(solution)/shard_map/all_gather | solution.py:28
  63.7 0.5 broadcast_in_dim.2
  64.2 9.1 %fusion.1 = bf16[2048,512]{0,1:T(8,128)(2,1)} fusion(bf16[2048,1792]{1,0:T(8,128)(2,1)} %all-gather.5.cloned.1.call-done, bf16[512,1792]{0,1:T(8,128)(2,1)} %copy.15, bf16[224,8,4,128]{3,2,1,0:T(4,128)(2,1)S(1)} %bitcast.23), kind=kOutput, calls=%fused_computation.4 | convolution fusion | flops 3760062464 | bytes 13107200 | tf_op jit(solution)/shard_map/dot_general | solution.py:29
  73.3 4.0 %copy.21 = bf16[2048,512]{1,0:T(8,128)(2,1)} copy(bf16[2048,512]{0,1:T(8,128)(2,1)} %fusion.1) | data formatting | bytes 4194304
  77.3 0.0 reduce-scatter.9.cloned.1.call-update
  77.3 0.2 reduce-scatter.7.cloned.1.call-start
  77.5 35.6 %all-gather.3.cloned.1.call-done = bf16[2048,512]{1,0:T(8,128)(2,1)} async-done(((bf16[128,512]{1,0:T(8,128)(2,1)}), bf16[2048,512]{1,0:T(8,128)(2,1)}) %all-gather.3.cloned.1.call-update) | async-done | bytes 2097168 | tf_op jit(solution)/shard_map/all_gather | solution.py:19
  113.1 9.1 %fusion = bf16[2048,1792]{0,1:T(8,128)(2,1)} fusion(bf16[2048,512]{1,0:T(8,128)(2,1)} %all-gather.3.cloned.1.call-done, bf16[512,1792]{0,1:T(8,128)(2,1)} %copy.15, bf16[224,8,4,128]{3,2,1,0:T(4,128)(2,1)S(1)} %bitcast.24), kind=kOutput, calls=%fused_computation.1 | convolution fusion | flops 3762683904 | bytes 13107200 | tf_op jit(solution)/shard_map/dot_general | solution.py:23
  122.2 10.1 %copy.19 = bf16[2048,1792]{1,0:T(8,128)(2,1)} copy(bf16[2048,1792]{0,1:T(8,128)(2,1)} %fusion) | data formatting | bytes 14680064
  132.3 0.0 reduce-scatter.7.cloned.1.call-update
  132.3 1.5 copy.31
  133.9 2.8 %copy.16 = bf16[512,1792]{1,0:T(8,128)(2,1)S(1)} copy(bf16[512,1792]{0,1:T(8,128)(2,1)} %bitcast.26) | data formatting | bytes 3670016 | tf_op jit(solution)/shard_map/reshape | solution.py:13
  136.7 9.1 %multiply_convert_fusion = bf16[512,1792]{1,0:T(8,128)(2,1)} fusion(bf16[512,1792]{1,0:T(8,128)(2,1)S(1)} %copy.16, bf16[2048,512]{1,0:T(8,128)(2,1)} %all-gather.3.cloned.1.call-done, bf16[2048,1792]{1,0:T(8,128)(2,1)} %all-gather.5.cloned.1.call-done), kind=kOutput, calls=%fused_computation.2 | convolution fusion | flops 3761766400 | bytes 13107200 | tf_op jit(solution)/shard_map/dot_general | solution.py:34
  145.8 50.3 %reduce-scatter.9.cloned.1.call-done = bf16[128,512]{1,0:T(8,128)(2,1)} async-done(((bf16[2048,512]{1,0:T(8,128)(2,1)}), bf16[128,512]{1,0:T(8,128)(2,1)}) %reduce-scatter.9.cloned.1.call-update) | async-done | bytes 131088
  196.1 72.7 %reduce-scatter.7.cloned.1.call-done = bf16[128,1792]{1,0:T(8,128)(2,1)} async-done(((bf16[2048,1792]{1,0:T(8,128)(2,1)}), bf16[128,1792]{1,0:T(8,128)(2,1)}) %reduce-scatter.7.cloned.1.call-update) | async-done | bytes 458768
Async XLA Ops:
  7.2 56.5 %all-gather.5.cloned.1.call-start = ((), (), s32[]{:S(2)}) async-start(), calls=%async_computation.3 | async-start | bytes 7798784 | tf_op jit(solution)/shard_map/all_gather | solution.py:28
  7.9 105.2 %all-gather.3.cloned.1.call-start = ((), (), s32[]{:S(2)}) async-start(), calls=%async_computation.2 | async-start | bytes 2228224 | tf_op jit(solution)/shard_map/all_gather | solution.py:19
  8.6 187.4 %reduce-scatter.9.cloned.1.call-start = ((), (), s32[]{:S(2)}) async-start(), calls=%async_computation.5 | async-start | bytes 2228224
  77.3 191.5 %reduce-scatter.7.cloned.1.call-start = ((), (), s32[]{:S(2)}) async-start(), calls=%async_computation.4 | async-start | bytes 7798784
Sparse Core Ops, SparseCore 0:
  9.8 53.8 all-gather.4
  66.1 46.9 all-gather.2
  117.3 78.7 reduce-scatter.8
  199.2 69.5 reduce-scatter.6
where the time goes:
time: 276 us; the launch traced here: 275 us
  waiting for transfers between devices  210 us (76%)
  matrix products  27.2 us (10%)
  local copies, waits for them, and re-layouts  22.8 us (8%)
  between operations  13.8 us (5%)
    unnamed x6, waiting for transfers between devices  124 us
    all_gather x1, waiting for transfers between devices, local(): shard_rows = lax.all_gather(cotangent, 'row', axis=0, tiled=True)  50.4 us
    all_gather x1, waiting for transfers between devices, local(): whole = lax.all_gather(inputs, 'col', axis=0, tiled=True)  35.6 us
    unnamed x4, local copies, waits for them, and re-layouts  19.4 us
    dot_general x1, matrix products, local(): jnp.dot(chosen, masked, preferred_element_type=jnp.float32)  9.1 us
    dot_general x1, matrix products, local(): lax.dot_general(chosen, shard_rows, (((0,), (0,)), ((), ())), preferred_e...  9.08 us
    dot_general x1, matrix products, local(): lax.dot_general(shard_rows, masked, (((1,), (1,)), ((), ())), preferred_e...  9.06 us
  transfers between devices with their start and end apart: 4, of which 4 were waited for; matrix products, arithmetic and copies ran while one was open for 18% of the time, Pallas kernels for 0%

commit v1 on v0

--- a/solution.py
+++ b/solution.py
@@ -16,7 +16,10 @@
 def local(inputs, weight, mask, cotangent):
     keep_mask = expand_mask(mask)
     masked = weight * keep_mask
-    whole = lax.all_gather(inputs, "col", axis=0, tiled=True)
+    n_dev = lax.axis_size("col")
+    blocks = jnp.stack([inputs for _ in range(n_dev)])
+    blocks = lax.all_to_all(blocks, "col", split_axis=0, concat_axis=0)
+    whole = jnp.concatenate(blocks, axis=0)
     token_total = whole.shape[0]
     chosen = whole
     outputs = lax.psum_scatter(

time: 276 us -> 226 us (0.82)
  waiting for transfers between devices: 210 us -> 152 us
  starting transfers between devices: 0.34 us -> 7.79 us
    all_gather x1, waiting for transfers between devices: 50.4 us -> 0.02 us  [local(): shard_rows = lax.all_gather(cotangent, 'row', axis=0, tiled=True)]
    all_gather x1 -> x0, waiting for transfers between devices: 35.6 us -> none  [local(): whole = lax.all_gather(inputs, 'col', axis=0, tiled=True)]
    all_to_all x0 -> x1, waiting for transfers between devices: none -> 24.4 us  [local(): blocks = lax.all_to_all(blocks, 'col', split_axis=0, concat_axis=0)]
    all_to_all x0 -> x1, starting transfers between devices: none -> 7.5 us  [local(): blocks = lax.all_to_all(blocks, 'col', split_axis=0, concat_axis=0)]
    unnamed x6 -> x5, waiting for transfers between devices: 124 us -> 127 us
    unnamed x4 -> x8, local copies, waits for them, and re-layouts: 19.4 us -> 17.9 us
  transfers between devices with their start and end apart: 4 -> 4, of which waited for: 4 -> 3; matrix products, arithmetic and copies ran while one was open for 18% -> 23% of each run, Pallas kernels for 0% -> 0%
where the time goes in v1:
time: 226 us; the launch traced here: 224 us
  waiting for transfers between devices  152 us (67%)
  matrix products  27.3 us (12%)
  local copies, waits for them, and re-layouts  23.9 us (11%)
  between operations  13.8 us (6%)
  starting transfers between devices  7.79 us (3%)
    unnamed x5, waiting for transfers between devices  127 us
    all_to_all x1, waiting for transfers between devices, local(): blocks = lax.all_to_all(blocks, 'col', split_axis=0, concat_axis=0)  24.4 us
    unnamed x8, local copies, waits for them, and re-layouts  17.9 us
    dot_general x1, matrix products, local(): jnp.dot(chosen, masked, preferred_element_type=jnp.float32)  9.17 us
    dot_general x1, matrix products, local(): lax.dot_general(chosen, shard_rows, (((0,), (0,)), ((), ())), preferred_e...  9.08 us
    dot_general x1, matrix products, local(): lax.dot_general(shard_rows, masked, (((1,), (1,)), ((), ())), preferred_e...  9.02 us
    all_to_all x1, starting transfers between devices, local(): blocks = lax.all_to_all(blocks, 'col', split_axis=0, concat_axis=0)  7.5 us
  transfers between devices with their start and end apart: 4, of which 3 were waited for; matrix products, arithmetic and copies ran while one was open for 23% of the time, Pallas kernels for 0%

profile of v1, /device:TPU:10, one launch (start us, length us, event | category | flops | bytes accessed | tf_op | source)
XLA Modules:
  0.0 224.4 jit_solution(13945207822689283063)
XLA Ops:
  7.2 0.0 all-gather.2.cloned.1.call-start
  7.2 0.7 all-gather.2.cloned.1.call-update
  7.9 2.5 %stack.2 = bf16[16,128,512]{2,1,0:T(8,128)(2,1)} broadcast(bf16[128,512]{1,0:T(8,128)(2,1)} %param.4), dimensions={1,2} | broadcast | bytes 2228224 | tf_op jit(solution)/shard_map/stack | solution.py:20
  10.4 7.5 %all-to-all-start = ((bf16[16,128,512]{2,1,0:T(8,128)(2,1)}), bf16[16,128,512]{2,1,0:T(8,128)(2,1)}, u32[]{:S(2)}, u32[]{:S(2)}) async-start(bf16[16,128,512]{2,1,0:T(8,128)(2,1)} %stack.2), calls=%async_computation | async-start | bytes 4194304 | tf_op jit(solution)/shard_map/all_to_all | solution.py:21
  17.9 0.0 reduce-scatter.7.cloned.1.call-start
  17.9 0.0 copy-done.1
  18.0 0.1 copy.14
  18.1 0.0 copy-done
  18.1 2.3 %copy.15 = bf16[512,1792]{0,1:T(8,128)(2,1)} copy(bf16[512,1792]{1,0:T(8,128)(2,1)S(1)} %copy-done) | data formatting | bytes 3670016 | tf_op args[1]
  20.4 24.4 %all-to-all-done = bf16[16,128,512]{2,1,0:T(8,128)(2,1)} async-done(((bf16[16,128,512]{2,1,0:T(8,128)(2,1)}), bf16[16,128,512]{2,1,0:T(8,128)(2,1)}, u32[]{:S(2)}, u32[]{:S(2)}) %all-to-all-start) | async-done | bytes 2097184 | tf_op jit(solution)/shard_map/all_to_all | solution.py:21
  44.7 0.5 broadcast_in_dim.2
  45.3 9.2 %fusion = bf16[2048,1792]{0,1:T(8,128)(2,1)} fusion(bf16[2048,512]{1,0:T(8,128)(2,1)} %bitcast, bf16[512,1792]{0,1:T(8,128)(2,1)} %copy.15, bf16[224,8,4,128]{3,2,1,0:T(4,128)(2,1)S(1)} %bitcast.24), kind=kOutput, calls=%fused_computation.1 | convolution fusion | flops 3762683904 | bytes 13107200 | tf_op jit(solution)/shard_map/dot_general | solution.py:26
  54.5 10.1 %copy.19 = bf16[2048,1792]{1,0:T(8,128)(2,1)} copy(bf16[2048,1792]{0,1:T(8,128)(2,1)} %fusion) | data formatting | bytes 14680064
  64.6 0.0 reduce-scatter.7.cloned.1.call-update
  64.6 0.2 reduce-scatter.9.cloned.1.call-start
  64.9 0.0 all-gather.2.cloned.1.call-done
  64.9 9.0 %fusion.1 = bf16[2048,512]{0,1:T(8,128)(2,1)} fusion(bf16[2048,1792]{1,0:T(8,128)(2,1)} %all-gather.2.cloned.1.call-done, bf16[512,1792]{0,1:T(8,128)(2,1)} %copy.15, bf16[224,8,4,128]{3,2,1,0:T(4,128)(2,1)S(1)} %bitcast.25), kind=kOutput, calls=%fused_computation.4 | convolution fusion | flops 3760062464 | bytes 13107200 | tf_op jit(solution)/shard_map/dot_general | solution.py:32
  73.9 3.9 %copy.21 = bf16[2048,512]{1,0:T(8,128)(2,1)} copy(bf16[2048,512]{0,1:T(8,128)(2,1)} %fusion.1) | data formatting | bytes 4194304
  77.8 0.0 reduce-scatter.9.cloned.1.call-update
  77.9 1.5 copy.31
  79.4 2.8 %copy.16 = bf16[512,1792]{1,0:T(8,128)(2,1)S(1)} copy(bf16[512,1792]{0,1:T(8,128)(2,1)} %bitcast.27) | data formatting | bytes 3670016 | tf_op jit(solution)/shard_map/reshape | solution.py:13
  82.3 9.1 %multiply_convert_fusion = bf16[512,1792]{1,0:T(8,128)(2,1)} fusion(bf16[512,1792]{1,0:T(8,128)(2,1)S(1)} %copy.16, bf16[2048,512]{1,0:T(8,128)(2,1)} %bitcast, bf16[2048,1792]{1,0:T(8,128)(2,1)} %all-gather.2.cloned.1.call-done), kind=kOutput, calls=%fused_computation.2 | convolution fusion | flops 3761766400 | bytes 13107200 | tf_op jit(solution)/shard_map/dot_general | solution.py:37
  91.3 45.9 %reduce-scatter.7.cloned.1.call-done = bf16[128,1792]{1,0:T(8,128)(2,1)} async-done(((bf16[2048,1792]{1,0:T(8,128)(2,1)}), bf16[128,1792]{1,0:T(8,128)(2,1)}) %reduce-scatter.7.cloned.1.call-update) | async-done | bytes 458768
  137.3 80.6 %reduce-scatter.9.cloned.1.call-done = bf16[128,512]{1,0:T(8,128)(2,1)} async-done(((bf16[2048,512]{1,0:T(8,128)(2,1)}), bf16[128,512]{1,0:T(8,128)(2,1)}) %reduce-scatter.9.cloned.1.call-update) | async-done | bytes 131088
  (3 shorter events, 0.0 us)
Async XLA Ops:
  7.2 57.7 %all-gather.2.cloned.1.call-start = ((), (), s32[]{:S(2)}) async-start(), calls=%async_computation.3 | async-start | bytes 7798784 | tf_op jit(solution)/shard_map/all_gather | solution.py:31
  10.4 7.5 %copy-start.1 = (s32[4,14]{1,0:T(4,128)S(1)}, s32[4,14]{1,0:T(4,128)}, u32[]{:S(2)}) copy-start(s32[4,14]{1,0:T(4,128)} %param.6) | copy-start | bytes 676
  10.4 7.7 %copy-start = (bf16[512,1792]{1,0:T(8,128)(2,1)S(1)}, bf16[512,1792]{1,0:T(8,128)(2,1)}, u32[]{:S(2)}) copy-start(bf16[512,1792]{1,0:T(8,128)(2,1)} %param.5) | copy-start | bytes 5505028
  10.4 34.4 %all-to-all-start = ((bf16[16,128,512]{2,1,0:T(8,128)(2,1)}), bf16[16,128,512]{2,1,0:T(8,128)(2,1)}, u32[]{:S(2)}, u32[]{:S(2)}) async-start(bf16[16,128,512]{2,1,0:T(8,128)(2,1)} %stack.2), calls=%async_computation | async-start | bytes 4194304 | tf_op jit(solution)/shard_map/all_to_all | solution.py:21
  17.9 119.4 %reduce-scatter.7.cloned.1.call-start = ((), (), s32[]{:S(2)}) async-start(), calls=%async_computation.4 | async-start | bytes 7798784
  64.6 153.3 %reduce-scatter.9.cloned.1.call-start = ((), (), s32[]{:S(2)}) async-start(), calls=%async_computation.5 | async-start | bytes 2228224
Sparse Core Ops, SparseCore 0:
  9.8 53.8 all-gather.1
  66.8 70.3 reduce-scatter.6
  141.4 76.4 reduce-scatter.8
